TPU v7x, 256 devices: a whole 4x4x8 slice. The times are simulated.
256 devices in a mesh: pipe: 8 (over x, core), vocab: 32 (over z, y).
Axes of the slice: x: 4, y: 4, z: 8, core: 2. Of those that a mesh axis runs over, the one named last changes fastest.
Arguments:
- hidden: bfloat16 [8, 128, 4096], P('pipe'), may hold values from -60 to 60
- norm_gain: float32 [4096], replicated, may hold values from 0.5 to 1.5
- out_weight: bfloat16 [128256, 4096], P(('pipe', 'vocab')), may hold values from -4 to 4
- targets: int32 [8, 128], P('pipe'), may hold values from 0 to 128255
- loss_mask: int32 [8, 128], P('pipe'), may hold values from 0 to 1, as said below
- slot_position: int32 [8, 128], P('pipe'), may hold values from 0 to 127, each once within a row
- counts: int32 [8], replicated, may hold values from 1 to 128, 640 in all
- loss_scale: float32 [], replicated, may hold values from 4096 to 32768
Outputs:
- loss: float32 [], replicated
- grad_hidden: bfloat16 [8, 128, 4096], P('pipe')
Inputs may be any that keep to these rules, and one draw needn't show every extreme that they name: The 8 counts sum to exactly 640, and one of them equals 128. Each row of slot_position holds every number of 0 to 127 once. Each row of loss_mask holds at least 64 ones.
All inputs are finite; a program needn't handle non-finite values.
Results may differ from a plain program's by a relative error of at most 0.0034.
Values may be sent and summed in bfloat16 or wider, within the bound.
No kernel may reach another device: no remote copies, remote signals or barrier semaphores. Data moves between devices by JAX's collectives and lax.ppermute only.
A program may use at most 64 MiB of HBM per device.

v0:
```python
import functools
import jax
import jax.numpy as jnp
from jax import lax
from jax.sharding import Mesh
from jax.sharding import PartitionSpec as P

PIPE_VOCAB = ("pipe_0", "pipe_1", "vocab_0", "vocab_1")
PIPE = ("pipe_0", "pipe_1")
VOCAB = ("vocab_0", "vocab_1")
EPSILON = 1e-05


def one_axis_at_a_time(value, axes):
    return functools.reduce(lax.pmax, axes, value)


def over_axes(value, axes):
    for axis in axes:
        value = lax.psum(value, axis)
    return value


def rms_scale(values, norm_gain):
    mean_square = jnp.mean(values * values, axis=-1, keepdims=True)
    return values * lax.rsqrt(mean_square + EPSILON) * norm_gain


def pull_rows(rows, norm_gain, cotangent):
    pullback = jax.vjp(lambda values: rms_scale(values, norm_gain), rows)[1]
    return pullback(cotangent)[0].astype(jnp.bfloat16)


def softmax_stats(logits, local_target):
    row_top = one_axis_at_a_time(jnp.max(logits, axis=1), PIPE_VOCAB)
    local_total = jnp.sum(jnp.exp(logits - row_top[:, None]), axis=1)
    exp_total, target_logit = (
        over_axes(local_total, PIPE_VOCAB),
        over_axes(local_target, PIPE_VOCAB),
    )
    return (row_top + jnp.log(exp_total), target_logit)


def body(hidden, norm_gain, out_weight, targets, loss_mask, slot_position, counts, loss_scale):
    micro_slots = hidden.shape[1]
    model_width = hidden.shape[2]
    shard_words = out_weight.shape[0]
    offset = lax.axis_index(PIPE_VOCAB) * shard_words
    own_rows = hidden.reshape(micro_slots, model_width).astype(jnp.float32)
    own_normed = rms_scale(own_rows, norm_gain).astype(jnp.bfloat16)
    all_normed, all_targets, all_masks, all_positions = (
        lax.all_gather(own_normed, PIPE, axis=0, tiled=True),
        lax.all_gather(targets.reshape(micro_slots), PIPE, axis=0, tiled=True),
        lax.all_gather(loss_mask.reshape(micro_slots), PIPE, axis=0, tiled=True),
        lax.all_gather(slot_position.reshape(micro_slots), PIPE, axis=0, tiled=True),
    )
    rows_total = all_normed.shape[0]
    micro_index = jnp.arange(rows_total, dtype=jnp.int32) // micro_slots
    count_row = jnp.sum(
        jnp.where(
            micro_index[:, None] == jnp.arange(counts.shape[0], dtype=jnp.int32)[None, :],
            counts[None, :],
            0,
        ),
        axis=1,
    )
    inside = all_positions < count_row
    token_weight = jnp.where(inside & (all_masks == 1), 1.0, 0.0).astype(jnp.float32)
    weight_total = jnp.sum(token_weight)
    work_normed, work_targets, work_weight = (all_normed, all_targets, token_weight)
    logits = lax.dot_general(
        work_normed, out_weight, (((1,), (1,)), ((), ())), preferred_element_type=jnp.float32
    )
    is_target = (
        jnp.arange(shard_words, dtype=jnp.int32)[None, :] == (work_targets - offset)[:, None]
    )
    local_target = jnp.sum(jnp.where(is_target, logits, 0.0), axis=1)
    log_total, target_logit = softmax_stats(logits, local_target)
    loss = jnp.sum(work_weight * (log_total - target_logit)) / weight_total
    token_coef = loss_scale * work_weight / weight_total
    logit_grad = (
        (jnp.exp(logits - log_total[:, None]) - is_target.astype(jnp.float32)) * token_coef[:, None]
    ).astype(jnp.bfloat16)
    work_grad = jnp.dot(logit_grad, out_weight, preferred_element_type=jnp.float32)
    grad_cube = work_grad.reshape(rows_total // micro_slots, micro_slots, model_width)
    micro_grad = lax.psum_scatter(grad_cube, PIPE, scatter_dimension=0, tiled=True)
    summed = lax.psum(micro_grad, VOCAB)
    grad_out = pull_rows(own_rows, norm_gain, summed.reshape(micro_slots, model_width))
    return (loss, grad_out.reshape(1, micro_slots, model_width))


def solution(mesh):
    split = Mesh(mesh.devices.reshape(4, 2, 8, 4), ("pipe_0", "pipe_1", "vocab_0", "vocab_1"))
    return jax.shard_map(
        body,
        mesh=split,
        in_specs=(
            P(PIPE, None, None),
            P(),
            P(PIPE_VOCAB, None),
            P(PIPE, None),
            P(PIPE, None),
            P(PIPE, None),
            P(),
            P(),
        ),
        out_specs=(P(), P(PIPE, None, None)),
        check_vma=False,
    )
```

profile of v0, /device:TPU:2, one launch (start us, length us, event | category | flops | bytes accessed | tf_op | source)
XLA Modules:
  0.0 420.2 jit_solution(3627735221512694325)
XLA Ops:
  7.2 0.0 copy-start.3
  7.2 0.0 copy-start.4
  7.2 0.0 copy-start.5
  7.2 0.0 copy-start.6
  7.2 0.0 all-gather.5.cloned.1.call-start
  7.3 1.5 fusion.3
  8.8 2.5 fusion.5
  11.3 0.0 all-gather.5.cloned.1.call-update
  11.3 0.0 reduce-scatter.2.cloned.1.call-start
  12.0 0.0 copy-done.3
  12.1 10.0 %all-gather.2 = s32[1,1024]{1,0:T(1,128)S(1)} all-gather(s32[1,128]{1,0:T(1,128)S(1)} %copy-done.3), channel_id=4, replica_groups=mesh['pipe_0'=4,'pipe_1'=2,'vocab_0'=8,'vocab_1'=4] {'pipe_0','pipe_1'}, dimensions={1}, use_global_device_ids=true | all-gather | bytes 4608 | tf_op jit(solution)/shard_map/all_gather | solution.py:53
  22.1 0.0 copy-done.4
  22.1 8.7 %all-gather.1 = s32[1,1024]{1,0:T(1,128)S(1)} all-gather(s32[1,128]{1,0:T(1,128)S(1)} %copy-done.4), channel_id=3, replica_groups=mesh['pipe_0'=4,'pipe_1'=2,'vocab_0'=8,'vocab_1'=4] {'pipe_0','pipe_1'}, dimensions={1}, use_global_device_ids=true | all-gather | bytes 4608 | tf_op jit(solution)/shard_map/all_gather | solution.py:54
  30.8 0.0 copy-done.5
  30.8 8.7 %all-gather = s32[1,1024]{1,0:T(1,128)S(1)} all-gather(s32[1,128]{1,0:T(1,128)S(1)} %copy-done.5), channel_id=2, replica_groups=mesh['pipe_0'=4,'pipe_1'=2,'vocab_0'=8,'vocab_1'=4] {'pipe_0','pipe_1'}, dimensions={1}, use_global_device_ids=true | all-gather | bytes 4608 | tf_op jit(solution)/shard_map/all_gather | solution.py:55
  39.6 0.0 copy-done.6
  39.6 0.1 select_reduce_fusion.1
  39.7 26.2 %all-gather.5.cloned.1.call-done = bf16[1024,4096]{1,0:T(8,128)(2,1)} async-done(((bf16[128,4096]{1,0:T(8,128)(2,1)}), bf16[1024,4096]{1,0:T(8,128)(2,1)}) %all-gather.5.cloned.1.call-update) | async-done | bytes 8388624 | tf_op jit(solution)/shard_map/all_gather | solution.py:52
  65.9 8.2 %fusion.18 = (f32[1024]{0:T(1024)S(1)}, f32[1024,501]{0,1:T(8,128)S(1)}) fusion(bf16[1024,4096]{1,0:T(8,128)(2,1)} %all-gather.5.cloned.1.call-done, bf16[501,4096]{1,0:T(8,128)(2,1)} %param.10), kind=kOutput, calls=%fused_computation.41 | convolution fusion | flops 4203204608 | bytes 14548992 | tf_op jit(solution)/shard_map/dot_general | solution.py:71
  74.1 9.1 %pmax.28 = f32[1024]{0:T(1024)S(1)} all-reduce(f32[1024]{0:T(1024)S(1)} %get-tuple-element.16), channel_id=1, replica_groups=mesh['pipe_0'=4,'pipe_1'=2,'vocab_0'=8,'vocab_1'=4] {'pipe_0'}, use_global_device_ids=true, to_apply=%region_3.4 | all-reduce | flops 1024 | bytes 8192 | tf_op jit(solution)/shard_map/pmax | solution.py:15
  83.2 2.5 pmax.29
  85.6 17.4 %pmax.30 = f32[1024]{0:T(1024)S(1)} all-reduce(f32[1024]{0:T(1024)S(1)} %pmax.29), channel_id=1, replica_groups=mesh['pipe_0'=4,'pipe_1'=2,'vocab_0'=8,'vocab_1'=4] {'vocab_0'}, use_global_device_ids=true, to_apply=%region_5.6 | all-reduce | flops 1024 | bytes 8192 | tf_op jit(solution)/shard_map/pmax | solution.py:15
  103.1 10.5 %pmax.31 = f32[1024]{0:T(1024)S(1)} all-reduce(f32[1024]{0:T(1024)S(1)} %pmax.30), channel_id=1, replica_groups=mesh['pipe_0'=4,'pipe_1'=2,'vocab_0'=8,'vocab_1'=4] {'vocab_1'}, use_global_device_ids=true, to_apply=%region_6.7 | all-reduce | flops 1024 | bytes 8192 | tf_op jit(solution)/shard_map/pmax | solution.py:15
  113.5 0.5 select_reduce_fusion
  114.1 8.8 %all-reduce.2 = (f32[1024]{0:T(1024)S(1)}, f32[1024]{0:T(1024)S(1)}) all-reduce(f32[1024]{0:T(1024)S(1)} %get-tuple-element.3, f32[1024]{0:T(1024)S(1)} %get-tuple-element.2), channel_id=1, replica_groups=mesh['pipe_0'=4,'pipe_1'=2,'vocab_0'=8,'vocab_1'=4] {'pipe_0'}, use_global_device_ids=true, to_apply=%region_8.9 | all-reduce | flops 2048 | bytes 16384 | tf_op jit(solution)/shard_map/psum | solution.py:20
  122.9 2.5 all-reduce.3
  125.4 15.3 %all-reduce = (f32[1024]{0:T(1024)S(1)}, f32[1024]{0:T(1024)S(1)}) all-reduce(f32[1024]{0:T(1024)S(1)} %get-tuple-element.12, f32[1024]{0:T(1024)S(1)} %get-tuple-element.13), channel_id=1, replica_groups=mesh['pipe_0'=4,'pipe_1'=2,'vocab_0'=8,'vocab_1'=4] {'vocab_0'}, use_global_device_ids=true, to_apply=%region_10.11 | all-reduce | flops 2048 | bytes 16384 | tf_op jit(solution)/shard_map/psum | solution.py:20
  140.7 7.8 %all-reduce.1 = (f32[1024]{0:T(1024)S(1)}, f32[1024]{0:T(1024)S(1)}) all-reduce(f32[1024]{0:T(1024)S(1)} %get-tuple-element.6, f32[1024]{0:T(1024)S(1)} %get-tuple-element.7), channel_id=1, replica_groups=mesh['pipe_0'=4,'pipe_1'=2,'vocab_0'=8,'vocab_1'=4] {'vocab_1'}, use_global_device_ids=true, to_apply=%region_11.12 | all-reduce | flops 2048 | bytes 16384 | tf_op jit(solution)/shard_map/psum | solution.py:20
  148.5 0.6 select_reduce_fusion.2
  149.1 0.7 fusion.13
  149.8 10.4 %fusion.8 = f32[1024,4096]{1,0:T(8,128)} fusion(bf16[501,4096]{1,0:T(8,128)(2,1)} %param.10, f32[1024,501]{0,1:T(8,128)S(1)} %get-tuple-element.17, f32[1024]{0:T(1024)S(1)} %fusion.13, f32[1024]{0:T(1024)S(1)} %get-tuple-element.14, s32[1024]{0:T(1024)S(1)} %bitcast.28), kind=kOutput, calls=%fused_computation.16 | convolution fusion | flops 4205770752 | bytes 22945792 | tf_op jit(solution)/shard_map/dot_general | solution.py:84
  160.2 0.0 reduce-scatter.2.cloned.1.call-update
  160.2 0.0 copy-start
  160.2 0.0 copy-start.2
  160.2 0.0 all-reduce.6.cloned.1.call-start
  160.3 88.6 %reduce-scatter.2.cloned.1.call-done = f32[1,128,4096]{2,1,0:T(8,128)} async-done(((f32[8,128,4096]{2,1,0:T(8,128)}), f32[1,128,4096]{2,1,0:T(8,128)}) %reduce-scatter.2.cloned.1.call-update) | async-done | bytes 2097168 | tf_op jit(solution)/shard_map/reduce_scatter | solution.py:86
  248.9 0.0 all-reduce.6.cloned.1.call-update
  250.2 158.6 %all-reduce.6.cloned.1.call-done = f32[1,128,4096]{2,1,0:T(8,128)} async-done(((f32[1,128,4096]{2,1,0:T(8,128)}), f32[1,128,4096]{2,1,0:T(8,128)}) %all-reduce.6.cloned.1.call-update) | async-done | bytes 2097168 | tf_op jit(solution)/shard_map/psum | solution.py:87
  408.8 0.0 copy-done
  408.8 0.0 copy-done.2
  408.8 0.0 copy-start.1
  408.8 2.1 fusion.6
  411.0 0.1 copy-done.1
  411.0 1.5 fusion.7
  (5 shorter events, 0.1 us)
Async XLA Ops:
  7.2 4.9 %copy-start.3 = (s32[1,128]{1,0:T(1,128)S(1)}, s32[1,128]{1,0:T(1,128)}, u32[]{:S(2)}) copy-start(s32[1,128]{1,0:T(1,128)} %param.11) | copy-start | bytes 1540
  7.2 14.9 %copy-start.4 = (s32[1,128]{1,0:T(1,128)S(1)}, s32[1,128]{1,0:T(1,128)}, u32[]{:S(2)}) copy-start(s32[1,128]{1,0:T(1,128)} %param.12) | copy-start | bytes 1540
  7.2 23.6 %copy-start.5 = (s32[1,128]{1,0:T(1,128)S(1)}, s32[1,128]{1,0:T(1,128)}, u32[]{:S(2)}) copy-start(s32[1,128]{1,0:T(1,128)} %param.13) | copy-start | bytes 1540
  7.2 32.4 %copy-start.6 = (s32[8]{0:T(128)S(1)}, s32[8]{0:T(128)}, u32[]{:S(2)}) copy-start(s32[8]{0:T(128)} %param.14) | copy-start | bytes 100
  7.2 58.7 %all-gather.5.cloned.1.call-start = ((), (), s32[]{:S(2)}) async-start(), calls=%async_computation.1 | async-start | bytes 9437184 | tf_op jit(solution)/shard_map/all_gather | solution.py:52
  11.3 237.5 %reduce-scatter.2.cloned.1.call-start = ((), (), s32[]{:S(2)}) async-start(), calls=%async_computation.2 | async-start | bytes 18874368 | tf_op jit(solution)/shard_map/reduce_scatter | solution.py:86
  160.2 248.6 %copy-start = (bf16[1,128,4096]{2,1,0:T(8,128)(2,1)S(1)}, bf16[1,128,4096]{2,1,0:T(8,128)(2,1)}, u32[]{:S(2)}) copy-start(bf16[1,128,4096]{2,1,0:T(8,128)(2,1)} %param.8) | copy-start | bytes 3145732
  160.2 248.6 %copy-start.2 = (f32[4096]{0:T(1024)S(1)}, f32[4096]{0:T(1024)}, u32[]{:S(2)}) copy-start(f32[4096]{0:T(1024)} %param.9) | copy-start | bytes 49156
  160.2 248.6 %all-reduce.6.cloned.1.call-start = ((), (), s32[]{:S(2)}) async-start(), calls=%async_computation.3 | async-start | bytes 4194304 | tf_op jit(solution)/shard_map/psum | solution.py:87
  408.8 2.2 copy-start.1
Sparse Core Ops, SparseCore 0:
  11.5 54.4 all-gather.4
  160.3 88.5 reduce-scatter.1
  252.4 156.3 all-reduce.5
where the time goes:
time: 421 us; the launch traced here: 420 us
  waiting for transfers between devices  273 us (65%)
  blocking collectives  101 us (24%)
  matrix products  18.5 us (4%)
  between operations  17 us (4%)
  other arithmetic  9.63 us (2%)
    psum x1, waiting for transfers between devices, body(): summed = lax.psum(micro_grad, VOCAB)  159 us
    reduce_scatter x1, waiting for transfers between devices, body(): lax.psum_scatter(grad_cube, PIPE, scatter_dimension=0, tiled=True)  88.6 us
    pmax x4, blocking collectives, one_axis_at_a_time(): return functools.reduce(lax.pmax, axes, value)  39.5 us
    psum x4, blocking collectives, over_axes(): value = lax.psum(value, axis)  34.4 us
    all_gather x1, waiting for transfers between devices, body(): lax.all_gather(own_normed, PIPE, axis=0, tiled=True)  26.2 us
    dot_general x1, matrix products, body(): jnp.dot(logit_grad, out_weight, preferred_element_type=jnp.float32)  10.4 us
    all_gather x1, blocking collectives, body(): lax.all_gather(targets.reshape(micro_slots), PIPE, axis=0, tiled=True)  10 us
    all_gather x1, blocking collectives, body(): lax.all_gather(loss_mask.reshape(micro_slots), PIPE, axis=0, tiled=True)  8.75 us
  transfers between devices with their start and end apart: 3, of which 3 were waited for; matrix products, arithmetic and copies ran while one was open for 0% of the time, Pallas kernels for 0%

commit v1 on v0

--- a/solution.py
+++ b/solution.py
@@ -17,7 +17,7 @@
 
 def over_axes(value, axes):
     for axis in axes:
-        value = lax.psum(value, axis)
+        value = jnp.sum(lax.all_gather(value, axis), axis=0)
     return value
 
 

time: 421 us -> 486 us (1.15)
  blocking collectives: 101 us -> 166 us
    all_gather x0 -> x8, blocking collectives: none -> 99 us  [over_axes(): value = jnp.sum(lax.all_gather(value, axis), axis=0)]
    psum x4 -> x0, blocking collectives: 34.4 us -> none  [over_axes(): value = lax.psum(value, axis)]
where the time goes in v1:
time: 486 us
  waiting for transfers between devices  274 us (56%)
  blocking collectives  166 us (34%)
  matrix products  18.5 us (4%)
  between operations  17 us (3%)
  other arithmetic  9.76 us (2%)
    psum x1, waiting for transfers between devices, body(): summed = lax.psum(micro_grad, VOCAB)  159 us
    all_gather x8, blocking collectives, over_axes(): value = jnp.sum(lax.all_gather(value, axis), axis=0)  99 us
    reduce_scatter x1, waiting for transfers between devices, body(): lax.psum_scatter(grad_cube, PIPE, scatter_dimension=0, tiled=True)  89.2 us
    pmax x4, blocking collectives, one_axis_at_a_time(): return functools.reduce(lax.pmax, axes, value)  39.5 us
    all_gather x1, waiting for transfers between devices, body(): lax.all_gather(own_normed, PIPE, axis=0, tiled=True)  26.2 us
    dot_general x1, matrix products, body(): jnp.dot(logit_grad, out_weight, preferred_element_type=jnp.float32)  10.4 us
    all_gather x1, blocking collectives, body(): lax.all_gather(targets.reshape(micro_slots), PIPE, axis=0, tiled=True)  10 us
  transfers between devices with their start and end apart: 3, of which 3 were waited for; matrix products, arithmetic and copies ran while one was open for 0% of the time, Pallas kernels for 0%

profile of v1, /device:TPU:2, one launch (start us, length us, event | category | flops | bytes accessed | tf_op | source)
XLA Modules:
  0.0 485.6 jit_solution(9869060572025981012)
XLA Ops:
  7.2 0.0 copy-start.3
  7.2 0.0 copy-start.4
  7.2 0.0 copy-start.5
  7.2 0.0 copy-start.6
  7.2 0.0 all-gather.13.cloned.1.call-start
  7.3 1.5 fusion.3
  8.8 2.5 fusion.5
  11.3 0.0 all-gather.13.cloned.1.call-update
  11.3 0.0 reduce-scatter.2.cloned.1.call-start
  12.0 0.0 copy-done.3
  12.1 10.0 %all-gather.6 = s32[1,1024]{1,0:T(1,128)S(1)} all-gather(s32[1,128]{1,0:T(1,128)S(1)} %copy-done.3), channel_id=8, replica_groups=mesh['pipe_0'=4,'pipe_1'=2,'vocab_0'=8,'vocab_1'=4] {'pipe_0','pipe_1'}, dimensions={1}, use_global_device_ids=true | all-gather | bytes 4608 | tf_op jit(solution)/shard_map/all_gather | solution.py:53
  22.1 0.0 copy-done.4
  22.1 8.7 %all-gather.1 = s32[1,1024]{1,0:T(1,128)S(1)} all-gather(s32[1,128]{1,0:T(1,128)S(1)} %copy-done.4), channel_id=3, replica_groups=mesh['pipe_0'=4,'pipe_1'=2,'vocab_0'=8,'vocab_1'=4] {'pipe_0','pipe_1'}, dimensions={1}, use_global_device_ids=true | all-gather | bytes 4608 | tf_op jit(solution)/shard_map/all_gather | solution.py:54
  30.8 0.0 copy-done.5
  30.8 8.7 %all-gather = s32[1,1024]{1,0:T(1,128)S(1)} all-gather(s32[1,128]{1,0:T(1,128)S(1)} %copy-done.5), channel_id=2, replica_groups=mesh['pipe_0'=4,'pipe_1'=2,'vocab_0'=8,'vocab_1'=4] {'pipe_0','pipe_1'}, dimensions={1}, use_global_device_ids=true | all-gather | bytes 4608 | tf_op jit(solution)/shard_map/all_gather | solution.py:55
  39.6 0.0 copy-done.6
  39.6 0.1 select_reduce_fusion.1
  39.7 26.2 %all-gather.13.cloned.1.call-done = bf16[1024,4096]{1,0:T(8,128)(2,1)} async-done(((bf16[128,4096]{1,0:T(8,128)(2,1)}), bf16[1024,4096]{1,0:T(8,128)(2,1)}) %all-gather.13.cloned.1.call-update) | async-done | bytes 8388624 | tf_op jit(solution)/shard_map/all_gather | solution.py:52
  65.9 8.2 %fusion.18 = (f32[1024]{0:T(1024)S(1)}, f32[1024,501]{0,1:T(8,128)S(1)}) fusion(bf16[1024,4096]{1,0:T(8,128)(2,1)} %all-gather.13.cloned.1.call-done, bf16[501,4096]{1,0:T(8,128)(2,1)} %param.10), kind=kOutput, calls=%fused_computation.41 | convolution fusion | flops 4203204608 | bytes 14548992 | tf_op jit(solution)/shard_map/dot_general | solution.py:71
  74.1 9.1 %pmax.28 = f32[1024]{0:T(1024)S(1)} all-reduce(f32[1024]{0:T(1024)S(1)} %get-tuple-element.8), channel_id=1, replica_groups=mesh['pipe_0'=4,'pipe_1'=2,'vocab_0'=8,'vocab_1'=4] {'pipe_0'}, use_global_device_ids=true, to_apply=%region_3.4 | all-reduce | flops 1024 | bytes 8192 | tf_op jit(solution)/shard_map/pmax | solution.py:15
  83.2 2.5 pmax.29
  85.6 17.4 %pmax.30 = f32[1024]{0:T(1024)S(1)} all-reduce(f32[1024]{0:T(1024)S(1)} %pmax.29), channel_id=1, replica_groups=mesh['pipe_0'=4,'pipe_1'=2,'vocab_0'=8,'vocab_1'=4] {'vocab_0'}, use_global_device_ids=true, to_apply=%region_5.6 | all-reduce | flops 1024 | bytes 8192 | tf_op jit(solution)/shard_map/pmax | solution.py:15
  103.1 10.5 %pmax.31 = f32[1024]{0:T(1024)S(1)} all-reduce(f32[1024]{0:T(1024)S(1)} %pmax.30), channel_id=1, replica_groups=mesh['pipe_0'=4,'pipe_1'=2,'vocab_0'=8,'vocab_1'=4] {'vocab_1'}, use_global_device_ids=true, to_apply=%region_6.7 | all-reduce | flops 1024 | bytes 8192 | tf_op jit(solution)/shard_map/pmax | solution.py:15
  113.5 0.5 select_reduce_fusion
  114.1 10.7 %all-gather.7 = f32[4096]{0:T(1024)S(1)} all-gather(f32[1024]{0:T(1024)S(1)} %get-tuple-element.2), channel_id=9, replica_groups=mesh['pipe_0'=4,'pipe_1'=2,'vocab_0'=8,'vocab_1'=4] {'pipe_0'}, dimensions={0}, use_global_device_ids=true | all-gather | bytes 20480 | tf_op jit(solution)/shard_map/all_gather | solution.py:20
  124.8 1.8 all-gather.8
  126.7 11.9 %all-gather.2 = f32[4096]{0:T(1024)S(1)} all-gather(f32[1024]{0:T(1024)S(1)} %get-tuple-element.3), channel_id=4, replica_groups=mesh['pipe_0'=4,'pipe_1'=2,'vocab_0'=8,'vocab_1'=4] {'pipe_0'}, dimensions={0}, use_global_device_ids=true | all-gather | bytes 20480 | tf_op jit(solution)/shard_map/all_gather | solution.py:20
  138.6 1.8 all-gather.3
  140.5 24.5 %all-gather.4 = f32[8192]{0:T(1024)S(1)} all-gather(f32[1024]{0:T(1024)S(1)} %reduce_sum.147), channel_id=6, replica_groups=mesh['pipe_0'=4,'pipe_1'=2,'vocab_0'=8,'vocab_1'=4] {'vocab_0'}, dimensions={0}, use_global_device_ids=true | all-gather | bytes 36864 | tf_op jit(solution)/shard_map/all_gather | solution.py:20
  165.0 11.9 %all-gather.5 = f32[4096]{0:T(1024)S(1)} all-gather(f32[1024]{0:T(1024)S(1)} %reduce_sum.148), channel_id=7, replica_groups=mesh['pipe_0'=4,'pipe_1'=2,'vocab_0'=8,'vocab_1'=4] {'vocab_1'}, dimensions={0}, use_global_device_ids=true | all-gather | bytes 20480 | tf_op jit(solution)/shard_map/all_gather | solution.py:20
  176.9 24.5 %all-gather.9 = f32[8192]{0:T(1024)S(1)} all-gather(f32[1024]{0:T(1024)S(1)} %reduce_sum.152), channel_id=11, replica_groups=mesh['pipe_0'=4,'pipe_1'=2,'vocab_0'=8,'vocab_1'=4] {'vocab_0'}, dimensions={0}, use_global_device_ids=true | all-gather | bytes 36864 | tf_op jit(solution)/shard_map/all_gather | solution.py:20
  201.4 11.9 %all-gather.10 = f32[4096]{0:T(1024)S(1)} all-gather(f32[1024]{0:T(1024)S(1)} %reduce_sum.153), channel_id=12, replica_groups=mesh['pipe_0'=4,'pipe_1'=2,'vocab_0'=8,'vocab_1'=4] {'vocab_1'}, dimensions={0}, use_global_device_ids=true | all-gather | bytes 20480 | tf_op jit(solution)/shard_map/all_gather | solution.py:20
  213.4 0.6 select_reduce_fusion.2
  214.0 0.7 fusion.13
  214.7 10.4 %fusion.8 = f32[1024,4096]{1,0:T(8,128)} fusion(bf16[501,4096]{1,0:T(8,128)(2,1)} %param.10, f32[1024,501]{0,1:T(8,128)S(1)} %get-tuple-element.9, f32[1024]{0:T(1024)S(1)} %fusion.13, f32[1024]{0:T(1024)S(1)} %get-tuple-element.6, s32[1024]{0:T(1024)S(1)} %bitcast.28), kind=kOutput, calls=%fused_computation.16 | convolution fusion | flops 4205770752 | bytes 22945792 | tf_op jit(solution)/shard_map/dot_general | solution.py:84
  225.0 0.0 reduce-scatter.2.cloned.1.call-update
  225.1 0.0 copy-start
  225.1 0.0 copy-start.2
  225.1 0.0 all-reduce.2.cloned.1.call-start
  225.1 89.2 %reduce-scatter.2.cloned.1.call-done = f32[1,128,4096]{2,1,0:T(8,128)} async-done(((f32[8,128,4096]{2,1,0:T(8,128)}), f32[1,128,4096]{2,1,0:T(8,128)}) %reduce-scatter.2.cloned.1.call-update) | async-done | bytes 2097168 | tf_op jit(solution)/shard_map/reduce_scatter | solution.py:86
  314.3 0.0 all-reduce.2.cloned.1.call-update
  315.7 158.6 %all-reduce.2.cloned.1.call-done = f32[1,128,4096]{2,1,0:T(8,128)} async-done(((f32[1,128,4096]{2,1,0:T(8,128)}), f32[1,128,4096]{2,1,0:T(8,128)}) %all-reduce.2.cloned.1.call-update) | async-done | bytes 2097168 | tf_op jit(solution)/shard_map/psum | solution.py:87
  474.2 0.0 copy-done
  474.2 0.0 copy-done.2
  474.2 0.0 copy-start.1
  474.2 2.1 fusion.6
  476.4 0.1 copy-done.1
  476.4 1.5 fusion.7
  (21 shorter events, 0.3 us)
Async XLA Ops:
  7.2 4.9 %copy-start.3 = (s32[1,128]{1,0:T(1,128)S(1)}, s32[1,128]{1,0:T(1,128)}, u32[]{:S(2)}) copy-start(s32[1,128]{1,0:T(1,128)} %param.11) | copy-start | bytes 1540
  7.2 14.9 %copy-start.4 = (s32[1,128]{1,0:T(1,128)S(1)}, s32[1,128]{1,0:T(1,128)}, u32[]{:S(2)}) copy-start(s32[1,128]{1,0:T(1,128)} %param.12) | copy-start | bytes 1540
  7.2 23.6 %copy-start.5 = (s32[1,128]{1,0:T(1,128)S(1)}, s32[1,128]{1,0:T(1,128)}, u32[]{:S(2)}) copy-start(s32[1,128]{1,0:T(1,128)} %param.13) | copy-start | bytes 1540
  7.2 32.4 %copy-start.6 = (s32[8]{0:T(128)S(1)}, s32[8]{0:T(128)}, u32[]{:S(2)}) copy-start(s32[8]{0:T(128)} %param.14) | copy-start | bytes 100
  7.2 58.7 %all-gather.13.cloned.1.call-start = ((), (), s32[]{:S(2)}) async-start(), calls=%async_computation.1 | async-start | bytes 9437184 | tf_op jit(solution)/shard_map/all_gather | solution.py:52
  11.3 303.0 %reduce-scatter.2.cloned.1.call-start = ((), (), s32[]{:S(2)}) async-start(), calls=%async_computation.2 | async-start | bytes 18874368 | tf_op jit(solution)/shard_map/reduce_scatter | solution.py:86
  225.1 249.2 %copy-start = (bf16[1,128,4096]{2,1,0:T(8,128)(2,1)S(1)}, bf16[1,128,4096]{2,1,0:T(8,128)(2,1)}, u32[]{:S(2)}) copy-start(bf16[1,128,4096]{2,1,0:T(8,128)(2,1)} %param.8) | copy-start | bytes 3145732
  225.1 249.2 %copy-start.2 = (f32[4096]{0:T(1024)S(1)}, f32[4096]{0:T(1024)}, u32[]{:S(2)}) copy-start(f32[4096]{0:T(1024)} %param.9) | copy-start | bytes 49156
  225.1 249.1 %all-reduce.2.cloned.1.call-start = ((), (), s32[]{:S(2)}) async-start(), calls=%async_computation.3 | async-start | bytes 4194304 | tf_op jit(solution)/shard_map/psum | solution.py:87
  474.2 2.2 copy-start.1
Sparse Core Ops, SparseCore 0:
  11.5 54.4 all-gather.12
  225.2 89.0 reduce-scatter.1
  317.8 156.3 all-reduce.1
